TPU v7x, 512 devices: a whole 4x4x16 slice. The times are simulated.
512 devices in a mesh: shard: 16 (over x_lo, y, core), loop: 32 (over x_hi, z).
Axes of the slice: x: 4 (x_hi: 2, x_lo: 2; x = x_hi * 2 + x_lo), y: 4, z: 16, core: 2. Of those that a mesh axis runs over, the one named last changes fastest.
Arguments:
- hidden: bfloat16 [983040, 768], P(('shard', 'loop')), may hold values from -6 to 6
- segment: int32 [983040], P(('shard', 'loop')), may hold values from 0 to 8, as said below
- counts: int32 [4096], P(('shard', 'loop')), may hold values from 1 to 720, as said below
- w_proj: bfloat16 [768, 128], replicated, may hold values from -0.21875 to 0.21875
- seeds: bfloat16 [256, 32, 128], P('loop', 'shard'), may hold values from -6 to 6
Outputs:
- scores: float32 [4096, 256], P(('shard', 'loop'))
Inputs may be any that keep to these rules, and one draw needn't show every extreme that they name: On every device one document has exactly 720 tokens, and a device's counts sum to less than 1920. `segment`: within a device, document k occupies counts of that document consecutive slots, documents in order of k from the first slot; all later slots hold 8, and every device has at least one such slot.
All inputs are finite; a program needn't handle non-finite values.
Results may differ from a plain program's by a relative error of at most 0.00055.
Values may be sent and summed in bfloat16 or wider, within the bound.
A program may use at most 64 MiB of HBM per device.

v0:
```python
import jax
import jax.numpy as jnp
from jax import lax
from jax.sharding import PartitionSpec as P

BETA = 16.0
EPS = 1e-06


def unit_rows(values):
    values = values.astype(jnp.float32)
    return (values * lax.rsqrt(jnp.sum(values * values, axis=-1, keepdims=True) + EPS)).astype(
        jnp.bfloat16
    )


def body(hidden, segment, counts, w_proj, seeds):
    projected = jnp.dot(hidden, w_proj, preferred_element_type=jnp.float32)
    doc_vectors = unit_rows(projected)
    doc_count = counts.shape[0]
    member = (segment[None, :] == jnp.arange(doc_count, dtype=jnp.int32)[:, None]).astype(
        jnp.bfloat16
    )
    lengths = counts.astype(jnp.float32)[:, None]
    own_seeds = lax.all_gather(unit_rows(seeds), "shard", axis=1, tiled=True)
    group = own_seeds.shape[0]
    qtokens = own_seeds.shape[1]
    width = own_seeds.shape[2]

    def score_group(block):
        flat = block.reshape(group * qtokens, width)
        sims = lax.dot_general(
            doc_vectors, flat, (((1,), (1,)), ((), ())), preferred_element_type=jnp.float32
        )
        weights = jnp.exp(BETA * sims)
        upper = weights.astype(jnp.bfloat16)
        lower = (weights - upper.astype(jnp.float32)).astype(jnp.bfloat16)
        mass = jnp.dot(member, upper, preferred_element_type=jnp.float32) + jnp.dot(
            member, lower, preferred_element_type=jnp.float32
        )
        logs = jnp.log(mass / lengths).reshape(doc_count, group, qtokens)
        return jnp.mean(logs, axis=-1)

    piece = lax.all_gather(own_seeds, "loop", axis=0, tiled=True)
    groups_here = piece.shape[0] // group
    result = lax.map(score_group, piece.reshape(groups_here, group, qtokens, width))
    return jnp.transpose(result, (1, 0, 2)).reshape(doc_count, groups_here * group)


def solution(mesh):
    in_specs = (
        P(("shard", "loop"), None),
        P(("shard", "loop")),
        P(("shard", "loop")),
        P(),
        P("loop", "shard", None),
    )
    out_specs = P(("shard", "loop"), None)
    return jax.shard_map(body, mesh=mesh, in_specs=in_specs, out_specs=out_specs, check_vma=False)
```

profile of v0, /device:TPU:16, one launch (start us, length us, event | category | flops | bytes accessed | tf_op | source)
XLA Modules:
  0.0 279.5 jit_solution(10549589936780741860)
XLA Ops:
  6.5 0.9 fusion.15
  8.2 18.2 %all_gather.6 = bf16[8,32,128]{2,0,1:T(8,128)(2,1)S(1)} all-gather(bf16[8,2,128]{2,0,1:T(8,128)(2,1)S(1)} %fusion.16), channel_id=1, replica_groups=mesh['shard'=16,'loop'=32] {'shard'}, dimensions={1}, use_global_device_ids=true | all-gather | bytes 69632 | tf_op jit(solution)/shard_map/all_gather | solution.py:25
  27.1 2.0 multiply_reduce_fusion
  30.0 1.3 copy.12
  31.3 149.0 %all-gather.2.cloned.1.call-done = bf16[256,32,128]{2,1,0:T(8,128)(2,1)} async-done(((bf16[8,32,128]{2,1,0:T(8,128)(2,1)}), bf16[256,32,128]{2,1,0:T(8,128)(2,1)}) %all-gather.2.cloned.1.call-update) | async-done | bytes 2097168 | tf_op jit(solution)/shard_map/all_gather | solution.py:44
  180.3 90.8 %while.11 = (s32[]{:T(128)}, f32[32,8,8]{2,1,0:T(8,128)}, bf16[32,8,32,128]{3,2,1,0:T(8,128)(2,1)}, bf16[1920,128]{1,0:T(8,128)(2,1)S(1)}, f32[8,1]{0,1:T(1,128)...) while((s32[]{:T(128)}, f32[32,8,8]{2,1,0:T(8,128)}, bf16[32,8,32,128]{3,2,1,0:T(8,128)(2,1)}, ...), condition=%wide.region_4.5_spmd.clone, body=%wide.region_2.4_spmd.clone.sunk | while | flops 144574464 | bytes 6656125 | solution.py:46
  180.3 0.8 constant_dynamic-slice_fusion.2
  183.1 0.8 constant_dynamic-slice_fusion.2
  185.9 0.8 constant_dynamic-slice_fusion.2
  188.8 0.8 constant_dynamic-slice_fusion.2
  191.6 0.8 constant_dynamic-slice_fusion.2
  194.5 0.8 constant_dynamic-slice_fusion.2
  197.3 0.8 constant_dynamic-slice_fusion.2
  200.1 0.8 constant_dynamic-slice_fusion.2
  203.0 0.8 constant_dynamic-slice_fusion.2
  205.8 0.8 constant_dynamic-slice_fusion.2
  208.6 0.8 constant_dynamic-slice_fusion.2
  211.5 0.8 constant_dynamic-slice_fusion.2
  214.3 0.8 constant_dynamic-slice_fusion.2
  217.1 0.8 constant_dynamic-slice_fusion.2
  220.0 0.8 constant_dynamic-slice_fusion.2
  222.8 0.8 constant_dynamic-slice_fusion.2
  225.7 0.8 constant_dynamic-slice_fusion.2
  228.5 0.8 constant_dynamic-slice_fusion.2
  231.3 0.8 constant_dynamic-slice_fusion.2
  234.2 0.8 constant_dynamic-slice_fusion.2
  237.0 0.8 constant_dynamic-slice_fusion.2
  239.8 0.8 constant_dynamic-slice_fusion.2
  242.7 0.8 constant_dynamic-slice_fusion.2
  262.5 0.8 constant_dynamic-slice_fusion.2
  265.4 0.8 constant_dynamic-slice_fusion.2
  271.0 0.9 copy.13
  (215 shorter events, 72.4 us)
Async XLA Ops:
  6.5 20.6 %copy-start = (bf16[1920,768]{1,0:T(8,128)(2,1)S(1)}, bf16[1920,768]{1,0:T(8,128)(2,1)}, u32[]{:S(2)}) copy-start(bf16[1920,768]{1,0:T(8,128)(2,1)} %param.7) | copy-start | bytes 8847364
  6.5 173.7 %all-gather.2.cloned.1.call-start = ((), (), s32[]{:S(2)}) async-start(), calls=%async_computation | async-start | bytes 2162688 | tf_op jit(solution)/shard_map/all_gather | solution.py:44
  29.1 2.2 copy-start.2
  29.1 151.2 %copy-start.1 = (s32[1920]{0:T(1024)S(1)}, s32[1920]{0:T(1024)}, u32[]{:S(2)}) copy-start(s32[1920]{0:T(1024)} %param.8) | copy-start | bytes 23044
Sparse Core Ops, SparseCore 0:
  27.2 153.0 all-gather.1
where the time goes:
time: 281 us; the launch traced here: 280 us
  waiting for transfers between devices  149 us (53%)
  matrix products  39 us (14%)
  local copies, waits for them, and re-layouts  34.7 us (12%)
  other arithmetic  24.9 us (9%)
  blocking collectives  18.2 us (6%)
  between operations  13.5 us (5%)
    all_gather x1, waiting for transfers between devices, body(): piece = lax.all_gather(own_seeds, 'loop', axis=0, tiled=True)  149 us
    dynamic_slice x32, local copies, waits for them, and re-layouts, body(): lax.map(score_group, piece.reshape(groups_here, group, qtokens, width))  27 us
    dynamic_update_slice x32, other arithmetic, body(): lax.map(score_group, piece.reshape(groups_here, group, qtokens, width))  19.5 us
    all_gather x1, blocking collectives, body(): own_seeds = lax.all_gather(unit_rows(seeds), 'shard', axis=1, tiled=True)  18.2 us
    dot_general x32, matrix products, score_group(): lax.dot_general(doc_vectors, flat, (((1,), (1,)), ((), ())), preferred_el...  14 us
    dot_general x32, matrix products, score_group(): jnp.dot(member, lower, preferred_element_type=jnp.float32)  12.8 us
    dot_general x32, matrix products, score_group(): jnp.dot(member, upper, preferred_element_type=jnp.float32)  10.2 us
  transfers between devices with their start and end apart: 1, of which 1 were waited for; matrix products, arithmetic and copies ran while one was open for 1% of the time, Pallas kernels for 0%

commit v1 on v0

v1 whole, which is shorter than its diff:
```python
import math

import jax
import jax.numpy as jnp
from jax import lax
from jax.experimental import pallas as pl
from jax.experimental.pallas import tpu as pltpu
from jax.sharding import PartitionSpec as P

BETA = 16.0
EPS = 1e-06
NX, NY, NZ = 4, 4, 16
ROWS, D_IN, D = 1920, 768, 128
SHARDS, LOOPS = 16, 32
MESH = pl.DeviceIdType.MESH
VMEM_LIMIT = 60 * 1024 * 1024


def unit_rows(values):
    values = values.astype(jnp.float32)
    return (values * lax.rsqrt(jnp.sum(values * values, axis=-1, keepdims=True) + EPS)).astype(
        jnp.bfloat16
    )


def gather_steps(own, buf, local_sem, send_z, recv_z, send_h, recv_h, send_c, recv_c):
    me_s = lax.axis_index("shard")
    me_l = lax.axis_index("loop")
    core, y, x_lo = me_s % 2, (me_s // 2) % NY, me_s // (2 * NY)
    x_hi, z = me_l // NZ, me_l % NZ
    x = 2 * x_hi + x_lo

    def device(px, py, pz, pc):
        return (((px % 2) * NY + py) * 2 + pc, (px // 2) * NZ + pz)

    def moved(value, by, size):
        return (value + by + size) % size

    def place(half, a, b, c, low=0, count=8):
        dx, dy = (a, b) if half == 0 else (b, a)
        px, py = moved(x, dx, NX), moved(y, dy, NY)
        return buf.at[((px % 2) * NY + py) * 2 + c, pl.ds((px // 2) * NZ + 8 * half + low, count)]

    def neighbour(half, order, by):
        if (half == 0) == (order == 0):
            return device(moved(x, by, NX), y, z, core)
        return device(x, moved(y, by, NY), z, core)

    barrier = pltpu.get_barrier_semaphore()
    partners = [device(x, y, moved(z, k, NZ), core) for k in range(1, NZ)]
    partners += [neighbour(0, 0, 1), neighbour(0, 0, -1), neighbour(0, 1, 1), neighbour(0, 1, -1)]
    partners += [device(x, y, z, 1 - core)]
    for partner in partners:
        pl.semaphore_signal(barrier, inc=1, device_id=partner, device_id_type=MESH)
    pl.semaphore_wait(barrier, len(partners))

    sent = []

    def remote(src, dst, send, recv, target):
        return pltpu.make_async_remote_copy(
            src_ref=src, dst_ref=dst, send_sem=send, recv_sem=recv, device_id=target, device_id_type=MESH
        )

    def z_copy(k, block):
        return remote(own, block, send_z.at[k], recv_z.at[k], device(x, y, moved(z, k, NZ), core))

    def start(copy):
        copy.start()
        sent.append(copy)

    mine = pltpu.make_async_copy(own, buf.at[me_s, me_l], local_sem)
    mine.start()
    for k in (8, 7, 9, 6, 10, 5, 11, 4, 12, 3, 13, 2, 14, 1, 15):
        start(z_copy(k, buf.at[me_s, me_l]))
    mine.wait()
    for k in range(1, NZ):
        z_copy(k, buf.at[me_s, x_hi * NZ + moved(z, -k, NZ)]).wait_recv()

    def hop(half, index, kind, ref, order):
        by = 1 if kind in (0, 2) else -1
        return remote(
            ref, ref, send_h.at[half, index, kind], recv_h.at[half, index, kind], neighbour(half, order, by)
        )

    def cross(half, a, b, c):
        ref = place(half, a, b, c)
        slot = (half * 4 + a % 4) * 4 + b % 4
        return remote(ref, ref, send_c.at[slot], recv_c.at[slot], device(x, y, z, 1 - core))

    def ready_first(half, a):
        start(hop(half, a % 4, 0, place(half, a, 0, core), 1))
        start(hop(half, a % 4, 1, place(half, a, 0, core), 1))
        start(cross(half, a, 0, core))

    halves = (0, 1)
    for half in halves:
        own_slab = place(half, 0, 0, core)
        start(hop(half, 4, 0, own_slab, 0))
        start(hop(half, 4, 1, own_slab, 0))
    for half in halves:
        ready_first(half, 0)
    for half in halves:
        hop(half, 4, 0, place(half, -1, 0, core), 0).wait_recv()
        start(hop(half, 4, 2, place(half, -1, 0, core, 0, 4), 0))
        hop(half, 4, 1, place(half, 1, 0, core), 0).wait_recv()
        start(hop(half, 4, 3, place(half, 1, 0, core, 4, 4), 0))
    for half in halves:
        ready_first(half, -1)
        ready_first(half, 1)

    def wait_second(half, a):
        hop(half, a % 4, 0, place(half, a, -1, core), 1).wait_recv()
        start(hop(half, a % 4, 2, place(half, a, -1, core, 0, 4), 1))
        hop(half, a % 4, 1, place(half, a, 1, core), 1).wait_recv()
        start(hop(half, a % 4, 3, place(half, a, 1, core, 4, 4), 1))
        start(cross(half, a, -1, core))
        start(cross(half, a, 1, core))

    for half in halves:
        hop(half, 4, 2, place(half, 2, 0, core, 0, 4), 0).wait_recv()
        hop(half, 4, 3, place(half, 2, 0, core, 4, 4), 0).wait_recv()
        ready_first(half, 2)
    for a in (0, -1, 1, 2):
        for half in halves:
            wait_second(half, a)
    for a in (0, -1, 1, 2):
        for half in halves:
            hop(half, a % 4, 2, place(half, a, 2, core, 0, 4), 1).wait_recv()
            hop(half, a % 4, 3, place(half, a, 2, core, 4, 4), 1).wait_recv()
            start(cross(half, a, 2, core))
    for b in (0, -1, 1, 2):
        for a in (0, -1, 1, 2):
            for half in halves:
                cross(half, a, b, 1 - core).wait_recv()
    for copy in sent:
        copy.wait_send()


def gather_kernel(own, out, buf, local_sem, send_z, recv_z, send_h, recv_h, send_c, recv_c):
    gather_steps(own, buf, local_sem, send_z, recv_z, send_h, recv_h, send_c, recv_c)
    final = pltpu.make_async_copy(buf, out, local_sem)
    final.start()
    final.wait()


def gather_blocks(block):
    dma = pltpu.SemaphoreType.DMA
    shape = (SHARDS, LOOPS) + block.shape
    return pl.pallas_call(
        gather_kernel,
        out_shape=jax.ShapeDtypeStruct(shape, block.dtype),
        in_specs=[pl.BlockSpec(memory_space=pltpu.VMEM)],
        out_specs=pl.BlockSpec(memory_space=pl.ANY),
        scratch_shapes=[
            pltpu.VMEM(shape, block.dtype),
            dma,
            dma((NZ,)),
            dma((NZ,)),
            dma((2, 5, 4)),
            dma((2, 5, 4)),
            dma((32,)),
            dma((32,)),
        ],
        compiler_params=pltpu.CompilerParams(collective_id=0, has_side_effects=True),
        name="seed_gather",
    )(block)


COLS = 512
CHUNKS = [(start, min(256, ROWS - start)) for start in range(0, ROWS, 256)]


def score_kernel(hidden, segment, counts, w_proj, seeds, out, vectors, member):
    for start in range(0, ROWS, 384):
        projected = jnp.dot(
            hidden[pl.ds(start, 384), :], w_proj[...], preferred_element_type=jnp.float32
        )
        vectors[pl.ds(start, 384), :] = unit_rows(projected)
    docs = lax.broadcasted_iota(jnp.int32, (16, ROWS), 0)
    member[...] = jnp.where(segment[...] == docs, 1.0, 0.0).astype(jnp.bfloat16)
    lengths = counts[...].astype(jnp.float32)

    def step(index, total):
        block = seeds[pl.ds(pl.multiple_of(index * COLS, COLS), COLS), :]
        mass = jnp.zeros((16, COLS), jnp.float32)
        for start, size in CHUNKS:
            sims = lax.dot_general(
                vectors[pl.ds(start, size), :],
                block,
                (((1,), (1,)), ((), ())),
                preferred_element_type=jnp.float32,
            )
            weights = jnp.exp2(sims * (BETA * math.log2(math.e))).astype(jnp.bfloat16)
            mass = mass + jnp.dot(
                member[:, pl.ds(start, size)], weights, preferred_element_type=jnp.float32
            )
        return total + jnp.log(mass[:8] / lengths)

    total = lax.fori_loop(0, SHARDS, step, jnp.zeros((8, COLS), jnp.float32))
    pairs = (
        lax.broadcasted_iota(jnp.int32, (COLS, COLS // 2), 0) // 2
        == lax.broadcasted_iota(jnp.int32, (COLS, COLS // 2), 1)
    ).astype(jnp.float32)
    out[...] = jnp.dot(
        total * (1.0 / 32.0), pairs, precision=lax.Precision.HIGHEST, preferred_element_type=jnp.float32
    )


def body(hidden, segment, counts, w_proj, seeds):
    block = unit_rows(seeds).reshape(16, D)
    gathered = gather_blocks(block).reshape(SHARDS * LOOPS * 16, D)
    return pl.pallas_call(
        score_kernel,
        out_shape=jax.ShapeDtypeStruct((8, 256), jnp.float32),
        scratch_shapes=[pltpu.VMEM((ROWS, D), jnp.bfloat16), pltpu.VMEM((16, ROWS), jnp.bfloat16)],
        compiler_params=pltpu.CompilerParams(vmem_limit_bytes=VMEM_LIMIT),
        name="soft_maxsim",
    )(hidden, segment.reshape(1, ROWS), counts.reshape(8, 1), w_proj, gathered)


def solution(mesh):
    in_specs = (
        P(("shard", "loop"), None),
        P(("shard", "loop")),
        P(("shard", "loop")),
        P(),
        P("loop", "shard", None),
    )
    out_specs = P(("shard", "loop"), None)
    return jax.shard_map(body, mesh=mesh, in_specs=in_specs, out_specs=out_specs, check_vma=False)
```

time: 281 us -> 83.2 us (0.30)
  the two profiles are of different devices: /device:TPU:16 before, /device:TPU:1 now
where the time goes in v1:
time: 83.2 us; the launch traced here: 82.9 us
  Pallas kernels  78.1 us (94%)
  local copies, waits for them, and re-layouts  2.61 us (3%)
  other arithmetic  2.14 us (3%)
    pallas_call x1, Pallas kernels, gather_blocks(): pl.pallas_call(gather_kernel, out_shape=jax.ShapeDtypeStruct(shape, block...  43.3 us
    pallas_call x1, Pallas kernels, body(): pl.pallas_call(score_kernel, out_shape=jax.ShapeDtypeStruct((8, 256), jnp...  34.9 us

profile of v1, /device:TPU:1, one launch (start us, length us, event | category | flops | bytes accessed | tf_op | source)
XLA Modules:
  0.0 82.9 jit_solution(2673984898900443061)
XLA Ops:
  0.0 1.3 %copy.6.counts = s32[8,1]{1,0:T(8,128)} copy(s32[8,1]{0,1:T(1,128)} %bitcast.5) | data formatting | bytes 64 | tf_op jit(solution)/shard_map/reshape | solution.py:218
  1.3 0.8 fusion
  2.1 1.4 %fusion.1 = bf16[8,2,128]{2,1,0:T(2,128)(2,1)} fusion(bf16[8,2,128]{2,1,0:T(2,128)(2,1)} %param.9, f32[8,2]{1,0:T(8,128)S(1)} %add_rsqrt_fusion), kind=kLoop, calls=%fused_computation.3 | loop fusion | flops 6144 | bytes 8256 | tf_op jit(solution)/shard_map/convert_element_type | solution.py:21
  3.5 1.3 %reshape.18.segment = s32[1,1920]{1,0:T(1,128)} reshape(s32[1920]{0:T(1024)} %param.6) | data formatting | bytes 15360 | tf_op jit(solution)/shard_map/reshape | solution.py:218
  4.8 43.3 %seed_gather.1 = bf16[16,32,16,128]{3,2,1,0:T(8,128)(2,1)} custom-call(bf16[16,128]{1,0:T(8,128)(2,1)} %bitcast.4), custom_call_target="tpu_custom_call" | custom-call | tf_op jit(solution)/shard_map/seed_gather/pallas_call | solution.py:149
  48.0 34.9 %soft_maxsim.1 = f32[8,256]{1,0:T(8,128)} custom-call(bf16[1920,768]{1,0:T(8,128)(2,1)} %hidden.1, s32[1,1920]{1,0:T(1,128)} %reshape.18.segment, s32[8,1]{1,0:T(8,128)} %copy.6.counts, bf16[768,128]{1,0:T(8,128)(2,1)} %w_proj.1, bf16[8192,128]{1,0:T(8,128)(2,1)} %bitcast.3), custom_call_target="tpu_custom_call" | custom-call | tf_op jit(solution)/shard_map/soft_maxsim/pallas_call | solution.py:212
  (1 shorter events, 0.0 us)

commit v2 on v1

--- a/solution.py
+++ b/solution.py
@@ -167,55 +167,109 @@
 
 
 COLS = 512
+LANES = 512
+PIECES = LANES // COLS
 CHUNKS = [(start, min(256, ROWS - start)) for start in range(0, ROWS, 256)]
 
 
-def score_kernel(hidden, segment, counts, w_proj, seeds, out, vectors, member):
+def similarity(vectors, block, start, size):
+    return lax.dot_general(
+        vectors[pl.ds(start, size), :],
+        block,
+        (((1,), (1,)), ((), ())),
+        preferred_element_type=jnp.float32,
+    )
+
+
+def overlapped(vectors, member, block, fill, drain):
+    mass = jnp.zeros((16, COLS), jnp.float32)
+    ahead = None
+    if fill is not None:
+        ahead = similarity(vectors, block, *CHUNKS[0])
+    for position, (start, size) in enumerate(CHUNKS):
+        now = ahead
+        if fill is not None and position + 1 < len(CHUNKS):
+            ahead = similarity(vectors, block, *CHUNKS[position + 1])
+        if drain is not None:
+            mass = mass + jnp.dot(
+                member[:, pl.ds(start, size)],
+                drain[pl.ds(start, size), :],
+                preferred_element_type=jnp.float32,
+            )
+        if fill is not None:
+            fill[pl.ds(start, size), :] = jnp.exp2(now * (BETA * math.log2(math.e))).astype(jnp.bfloat16)
+    return mass[:8]
+
+
+def score_kernel(hidden, counts, w_proj, seeds, out, vectors, member, totals, even, odd):
     for start in range(0, ROWS, 384):
         projected = jnp.dot(
             hidden[pl.ds(start, 384), :], w_proj[...], preferred_element_type=jnp.float32
         )
         vectors[pl.ds(start, 384), :] = unit_rows(projected)
     docs = lax.broadcasted_iota(jnp.int32, (16, ROWS), 0)
-    member[...] = jnp.where(segment[...] == docs, 1.0, 0.0).astype(jnp.bfloat16)
-    lengths = counts[...].astype(jnp.float32)
-
-    def step(index, total):
-        block = seeds[pl.ds(pl.multiple_of(index * COLS, COLS), COLS), :]
-        mass = jnp.zeros((16, COLS), jnp.float32)
-        for start, size in CHUNKS:
-            sims = lax.dot_general(
-                vectors[pl.ds(start, size), :],
-                block,
-                (((1,), (1,)), ((), ())),
-                preferred_element_type=jnp.float32,
-            )
-            weights = jnp.exp2(sims * (BETA * math.log2(math.e))).astype(jnp.bfloat16)
-            mass = mass + jnp.dot(
-                member[:, pl.ds(start, size)], weights, preferred_element_type=jnp.float32
-            )
-        return total + jnp.log(mass[:8] / lengths)
-
-    total = lax.fori_loop(0, SHARDS, step, jnp.zeros((8, COLS), jnp.float32))
+    slots = lax.broadcasted_iota(jnp.int32, (16, ROWS), 1)
+    rows = lax.broadcasted_iota(jnp.int32, (8, COLS), 0)
+    inside = jnp.zeros((16, ROWS), jnp.bool_)
+    lengths = jnp.ones((8, COLS), jnp.float32)
+    first = jnp.int32(0)
+    for doc in range(8):
+        last = first + counts[doc]
+        inside = inside | ((docs == doc) & (slots >= first) & (slots < last))
+        lengths = jnp.where(rows == doc, counts[doc].astype(jnp.float32), lengths)
+        first = last
+    member[...] = jnp.where(inside, 1.0, 0.0).astype(jnp.bfloat16)
+    totals[...] = jnp.zeros_like(totals)
+
+    def block_of(index):
+        return seeds[pl.ds(pl.multiple_of(index * COLS, COLS), COLS), :]
+
+    def add(index, mass):
+        totals[index % PIECES] += jnp.log(mass / lengths)
+
+    last = SHARDS * PIECES - 1
+    overlapped(vectors, member, block_of(0), even, None)
+
+    def step(pair, carry):
+        add(2 * pair, overlapped(vectors, member, block_of(2 * pair + 1), odd, even))
+        add(2 * pair + 1, overlapped(vectors, member, block_of(2 * pair + 2), even, odd))
+        return carry
+
+    lax.fori_loop(0, last // 2, step, 0)
+    add(last - 1, overlapped(vectors, member, block_of(last), odd, even))
+    add(last, overlapped(vectors, member, None, None, odd))
     pairs = (
         lax.broadcasted_iota(jnp.int32, (COLS, COLS // 2), 0) // 2
         == lax.broadcasted_iota(jnp.int32, (COLS, COLS // 2), 1)
     ).astype(jnp.float32)
-    out[...] = jnp.dot(
-        total * (1.0 / 32.0), pairs, precision=lax.Precision.HIGHEST, preferred_element_type=jnp.float32
-    )
+    for piece in range(PIECES):
+        out[:, pl.ds(piece * (COLS // 2), COLS // 2)] = jnp.dot(
+            totals[piece] * (1.0 / 32.0),
+            pairs,
+            precision=lax.Precision.HIGHEST,
+            preferred_element_type=jnp.float32,
+        )
 
 
 def body(hidden, segment, counts, w_proj, seeds):
     block = unit_rows(seeds).reshape(16, D)
     gathered = gather_blocks(block).reshape(SHARDS * LOOPS * 16, D)
+    vmem = pl.BlockSpec(memory_space=pltpu.VMEM)
     return pl.pallas_call(
         score_kernel,
         out_shape=jax.ShapeDtypeStruct((8, 256), jnp.float32),
-        scratch_shapes=[pltpu.VMEM((ROWS, D), jnp.bfloat16), pltpu.VMEM((16, ROWS), jnp.bfloat16)],
+        in_specs=[vmem, pl.BlockSpec(memory_space=pltpu.SMEM), vmem, vmem],
+        out_specs=vmem,
+        scratch_shapes=[
+            pltpu.VMEM((ROWS, D), jnp.bfloat16),
+            pltpu.VMEM((16, ROWS), jnp.bfloat16),
+            pltpu.VMEM((PIECES, 8, COLS), jnp.float32),
+            pltpu.VMEM((ROWS, COLS), jnp.bfloat16),
+            pltpu.VMEM((ROWS, COLS), jnp.bfloat16),
+        ],
         compiler_params=pltpu.CompilerParams(vmem_limit_bytes=VMEM_LIMIT),
         name="soft_maxsim",
-    )(hidden, segment.reshape(1, ROWS), counts.reshape(8, 1), w_proj, gathered)
+    )(hidden, counts, w_proj, gathered)
 
 
 def solution(mesh):

time: 83.2 us -> 65.7 us (0.79)
  Pallas kernels: 78.1 us -> 63.3 us
  local copies, waits for them, and re-layouts: 2.61 us -> 0 us
    pallas_call x1, Pallas kernels: 34.9 us -> 20.1 us  [body(): pl.pallas_call(score_kernel, out_shape=jax.ShapeDtypeStruct((8, 256), jnp...]
    reshape x2 -> x0, local copies, waits for them, and re-layouts: 2.61 us -> none  [the longest x1 1.32 us: body(): counts.reshape(8, 1)]
where the time goes in v2:
time: 65.7 us; the launch traced here: 65.5 us
  Pallas kernels  63.3 us (96%)
  other arithmetic  2.14 us (3%)
    pallas_call x1, Pallas kernels, gather_blocks(): pl.pallas_call(gather_kernel, out_shape=jax.ShapeDtypeStruct(shape, block...  43.3 us
    pallas_call x1, Pallas kernels, body(): pl.pallas_call(score_kernel, out_shape=jax.ShapeDtypeStruct((8, 256), jnp...  20.1 us
    convert_element_type x1, other arithmetic, unit_rows(): (values * lax.rsqrt(jnp.sum(values * values, axis=-1, keepdims=True) + EP...  1.36 us

profile of v2, /device:TPU:1, one launch (start us, length us, event | category | flops | bytes accessed | tf_op | source)
XLA Modules:
  0.0 65.5 jit_solution(11708988169869233042)
XLA Ops:
  0.0 0.8 %fusion = f32[8,2]{1,0:T(8,128)S(1)} fusion(bf16[8,2,128]{2,1,0:T(2,128)(2,1)} %param.8), kind=kLoop, calls=%fused_computation.2 | loop fusion | flops 6128 | bytes 4160 | tf_op jit(solution)/shard_map/reduce_sum | solution.py:21
  0.8 1.4 %fusion.1 = bf16[8,2,128]{2,1,0:T(2,128)(2,1)} fusion(bf16[8,2,128]{2,1,0:T(2,128)(2,1)} %param.8, f32[8,2]{1,0:T(8,128)S(1)} %add_rsqrt_fusion), kind=kLoop, calls=%fused_computation.3 | loop fusion | flops 6144 | bytes 8256 | tf_op jit(solution)/shard_map/convert_element_type | solution.py:21
  2.1 43.3 %seed_gather.1 = bf16[16,32,16,128]{3,2,1,0:T(8,128)(2,1)} custom-call(bf16[16,128]{1,0:T(8,128)(2,1)} %bitcast.3), custom_call_target="tpu_custom_call" | custom-call | tf_op jit(solution)/shard_map/seed_gather/pallas_call | solution.py:149
  45.4 20.1 %soft_maxsim.1 = f32[8,256]{1,0:T(8,128)} custom-call(bf16[1920,768]{1,0:T(8,128)(2,1)} %hidden.1, s32[8]{0:T(128)} %counts.1, bf16[768,128]{1,0:T(8,128)(2,1)} %w_proj.1, bf16[8192,128]{1,0:T(8,128)(2,1)} %bitcast.2), custom_call_target="tpu_custom_call" | custom-call | tf_op jit(solution)/shard_map/soft_maxsim/pallas_call | solution.py:258
  (1 shorter events, 0.0 us)

commit v3 on v1

v3 whole, which is shorter than its diff:
```python
import math

import jax
import jax.numpy as jnp
from jax import lax
from jax.experimental import pallas as pl
from jax.experimental.pallas import tpu as pltpu
from jax.sharding import PartitionSpec as P

BETA = 16.0
EPS = 1e-06
NX, NY, NZ = 4, 4, 16
ROWS, D_IN, D = 1920, 768, 128
SHARDS, LOOPS = 16, 32
MESH = pl.DeviceIdType.MESH
VMEM_LIMIT = 60 * 1024 * 1024


def unit_rows(values):
    values = values.astype(jnp.float32)
    return (values * lax.rsqrt(jnp.sum(values * values, axis=-1, keepdims=True) + EPS)).astype(
        jnp.bfloat16
    )


COLS = 512
CHUNKS = [(start, min(256, ROWS - start)) for start in range(0, ROWS, 256)]


def similarity(vectors, block, start, size):
    return lax.dot_general(
        vectors[pl.ds(start, size), :],
        block,
        (((1,), (1,)), ((), ())),
        preferred_element_type=jnp.float32,
    )


def overlapped(vectors, member, block, fill, drain):
    mass = jnp.zeros((16, COLS), jnp.float32)
    ahead = None
    if fill is not None:
        ahead = similarity(vectors, block, *CHUNKS[0])
    for position, (start, size) in enumerate(CHUNKS):
        now = ahead
        if fill is not None and position + 1 < len(CHUNKS):
            ahead = similarity(vectors, block, *CHUNKS[position + 1])
        if drain is not None:
            mass = mass + jnp.dot(
                member[:, pl.ds(start, size)],
                drain[pl.ds(start, size), :],
                preferred_element_type=jnp.float32,
            )
        if fill is not None:
            fill[pl.ds(start, size), :] = jnp.exp2(now * (BETA * math.log2(math.e))).astype(jnp.bfloat16)
    return mass[:8]


def prepare(hidden, counts, w_proj, vectors, member, totals):
    for start in range(0, ROWS, 384):
        projected = jnp.dot(
            hidden[pl.ds(start, 384), :], w_proj[...], preferred_element_type=jnp.float32
        )
        vectors[pl.ds(start, 384), :] = unit_rows(projected)
    docs = lax.broadcasted_iota(jnp.int32, (16, ROWS), 0)
    slots = lax.broadcasted_iota(jnp.int32, (16, ROWS), 1)
    rows = lax.broadcasted_iota(jnp.int32, (8, COLS), 0)
    inside = jnp.zeros((16, ROWS), jnp.bool_)
    lengths = jnp.ones((8, COLS), jnp.float32)
    first = jnp.int32(0)
    for doc in range(8):
        last = first + counts[doc]
        inside = inside | ((docs == doc) & (slots >= first) & (slots < last))
        lengths = jnp.where(rows == doc, counts[doc].astype(jnp.float32), lengths)
        first = last
    member[...] = jnp.where(inside, 1.0, 0.0).astype(jnp.bfloat16)
    totals[...] = jnp.zeros_like(totals)
    return lengths


def fused_kernel(
    own, hidden, counts, w_proj, out,
    buf, rows_in, vectors, member, totals, even, odd,
    local_sem, hidden_sem, send_z, recv_z, send_h, recv_h, send_c, recv_c,
):
    fetch = pltpu.make_async_copy(hidden, rows_in, hidden_sem)
    fetch.start()
    me_s = lax.axis_index("shard")
    me_l = lax.axis_index("loop")
    core, y, x_lo = me_s % 2, (me_s // 2) % NY, me_s // (2 * NY)
    x_hi, z = me_l // NZ, me_l % NZ
    x = 2 * x_hi + x_lo

    def device(px, py, pz, pc):
        return (((px % 2) * NY + py) * 2 + pc, (px // 2) * NZ + pz)

    def moved(value, by, size):
        return (value + by + size) % size

    def place(half, a, b, c, low=0, count=8):
        dx, dy = (a, b) if half == 0 else (b, a)
        px, py = moved(x, dx, NX), moved(y, dy, NY)
        return buf.at[((px % 2) * NY + py) * 2 + c, pl.ds((px // 2) * NZ + 8 * half + low, count)]

    def neighbour(half, order, by):
        if (half == 0) == (order == 0):
            return device(moved(x, by, NX), y, z, core)
        return device(x, moved(y, by, NY), z, core)

    barrier = pltpu.get_barrier_semaphore()
    partners = [device(x, y, moved(z, k, NZ), core) for k in range(1, NZ)]
    partners += [neighbour(0, 0, 1), neighbour(0, 0, -1), neighbour(0, 1, 1), neighbour(0, 1, -1)]
    partners += [device(x, y, z, 1 - core)]
    for partner in partners:
        pl.semaphore_signal(barrier, inc=1, device_id=partner, device_id_type=MESH)
    pl.semaphore_wait(barrier, len(partners))

    sent = []

    def remote(src, dst, send, recv, target):
        return pltpu.make_async_remote_copy(
            src_ref=src, dst_ref=dst, send_sem=send, recv_sem=recv, device_id=target, device_id_type=MESH
        )

    def z_copy(k, block):
        return remote(own, block, send_z.at[k], recv_z.at[k], device(x, y, moved(z, k, NZ), core))

    def start(copy):
        copy.start()
        sent.append(copy)

    mine = pltpu.make_async_copy(own, buf.at[me_s, me_l], local_sem)
    mine.start()
    for k in (8, 7, 9, 6, 10, 5, 11, 4, 12, 3, 13, 2, 14, 1, 15):
        start(z_copy(k, buf.at[me_s, me_l]))
    fetch.wait()
    lengths = prepare(rows_in, counts, w_proj, vectors, member, totals)
    mine.wait()
    for k in range(1, NZ):
        z_copy(k, buf.at[me_s, x_hi * NZ + moved(z, -k, NZ)]).wait_recv()

    def hop(half, index, kind, ref, order):
        by = 1 if kind in (0, 2) else -1
        return remote(
            ref, ref, send_h.at[half, index, kind], recv_h.at[half, index, kind], neighbour(half, order, by)
        )

    def cross(half, a, b, c):
        ref = place(half, a, b, c)
        slot = (half * 4 + a % 4) * 4 + b % 4
        return remote(ref, ref, send_c.at[slot], recv_c.at[slot], device(x, y, z, 1 - core))

    def ready_first(half, a):
        start(hop(half, a % 4, 0, place(half, a, 0, core), 1))
        start(hop(half, a % 4, 1, place(half, a, 0, core), 1))
        start(cross(half, a, 0, core))

    halves = (0, 1)
    slabs = [(half, side) for half in halves for side in (-1, 1)]

    def first_arrived(half):
        hop(half, 4, 0, place(half, -1, 0, core), 0).wait_recv()
        start(hop(half, 4, 2, place(half, -1, 0, core, 0, 4), 0))
        hop(half, 4, 1, place(half, 1, 0, core), 0).wait_recv()
        start(hop(half, 4, 3, place(half, 1, 0, core, 4, 4), 0))
        ready_first(half, -1)
        ready_first(half, 1)

    def first_opposite(half):
        hop(half, 4, 2, place(half, 2, 0, core, 0, 4), 0).wait_recv()
        hop(half, 4, 3, place(half, 2, 0, core, 4, 4), 0).wait_recv()
        ready_first(half, 2)

    def second_arrived(half, a):
        hop(half, a % 4, 0, place(half, a, -1, core), 1).wait_recv()
        start(hop(half, a % 4, 2, place(half, a, -1, core, 0, 4), 1))
        hop(half, a % 4, 1, place(half, a, 1, core), 1).wait_recv()
        start(hop(half, a % 4, 3, place(half, a, 1, core, 4, 4), 1))
        start(cross(half, a, -1, core))
        start(cross(half, a, 1, core))

    def second_opposite(half, a):
        hop(half, a % 4, 2, place(half, a, 2, core, 0, 4), 1).wait_recv()
        hop(half, a % 4, 3, place(half, a, 2, core, 4, 4), 1).wait_recv()
        start(cross(half, a, 2, core))

    scratch = (even, odd)
    done = []

    def drained(block, fill, drain):
        mass = overlapped(vectors, member, block, fill, drain)
        if drain is not None:
            totals[done[-1]] += jnp.log(mass / lengths)

    def score(dx, dy):
        cross(0, dx, dy, 1 - core).wait_recv()
        cross(1, dy, dx, 1 - core).wait_recv()
        px, py = moved(x, dx, NX), moved(y, dy, NY)
        block = buf[pl.ds(((px % 2) * NY + py) * 2, 2), pl.ds((px // 2) * NZ, NZ)].reshape(COLS, D)
        turn = len(done)
        drained(block, scratch[turn % 2], scratch[(turn - 1) % 2] if turn else None)
        done.append(px // 2)

    for half in halves:
        own_slab = place(half, 0, 0, core)
        start(hop(half, 4, 0, own_slab, 0))
        start(hop(half, 4, 1, own_slab, 0))
    for half in halves:
        ready_first(half, 0)
    score(0, 0)
    for half in halves:
        first_arrived(half)
    for half in halves:
        second_arrived(half, 0)
    score(1, 0)
    for half in halves:
        first_opposite(half)
    score(-1, 0)
    for half in halves:
        second_opposite(half, 0)
    score(0, 1)
    for half, side in slabs:
        second_arrived(half, side)
    score(0, -1)
    for half in halves:
        second_arrived(half, 2)
    score(2, 0)
    for half, side in slabs:
        second_opposite(half, side)
    score(0, 2)
    for half in halves:
        second_opposite(half, 2)
    for dx, dy in ((1, 1), (1, -1), (-1, 1), (-1, -1), (2, 1), (2, -1), (1, 2), (-1, 2), (2, 2)):
        score(dx, dy)
    drained(None, None, scratch[(len(done) - 1) % 2])
    pairs = (
        lax.broadcasted_iota(jnp.int32, (COLS // 2, COLS // 4), 0) // 2
        == lax.broadcasted_iota(jnp.int32, (COLS // 2, COLS // 4), 1)
    ).astype(jnp.float32)
    for side in range(2):
        both = totals[side][:, : COLS // 2] + totals[side][:, COLS // 2 :]
        out[:, pl.ds(side * (COLS // 4), COLS // 4)] = jnp.dot(
            both * (1.0 / 32.0),
            pairs,
            precision=lax.Precision.HIGHEST,
            preferred_element_type=jnp.float32,
        )
    for copy in sent:
        copy.wait_send()


def body(hidden, segment, counts, w_proj, seeds):
    block = unit_rows(seeds).reshape(16, D)
    vmem = pl.BlockSpec(memory_space=pltpu.VMEM)
    dma = pltpu.SemaphoreType.DMA
    return pl.pallas_call(
        fused_kernel,
        out_shape=jax.ShapeDtypeStruct((8, 256), jnp.float32),
        in_specs=[
            vmem,
            pl.BlockSpec(memory_space=pl.ANY),
            pl.BlockSpec(memory_space=pltpu.SMEM),
            vmem,
        ],
        out_specs=vmem,
        scratch_shapes=[
            pltpu.VMEM((SHARDS, LOOPS, 16, D), jnp.bfloat16),
            pltpu.VMEM((ROWS, D_IN), jnp.bfloat16),
            pltpu.VMEM((ROWS, D), jnp.bfloat16),
            pltpu.VMEM((16, ROWS), jnp.bfloat16),
            pltpu.VMEM((2, 8, COLS), jnp.float32),
            pltpu.VMEM((ROWS, COLS), jnp.bfloat16),
            pltpu.VMEM((ROWS, COLS), jnp.bfloat16),
            dma,
            dma,
            dma((NZ,)),
            dma((NZ,)),
            dma((2, 5, 4)),
            dma((2, 5, 4)),
            dma((32,)),
            dma((32,)),
        ],
        compiler_params=pltpu.CompilerParams(
            collective_id=0, has_side_effects=True, vmem_limit_bytes=VMEM_LIMIT
        ),
        name="gather_maxsim",
    )(block, hidden, counts, w_proj)


def solution(mesh):
    in_specs = (
        P(("shard", "loop"), None),
        P(("shard", "loop")),
        P(("shard", "loop")),
        P(),
        P("loop", "shard", None),
    )
    out_specs = P(("shard", "loop"), None)
    return jax.shard_map(body, mesh=mesh, in_specs=in_specs, out_specs=out_specs, check_vma=False)
```

time: 83.2 us -> 53.8 us (0.65)
  Pallas kernels: 78.1 us -> 50.1 us
  local copies, waits for them, and re-layouts: 2.61 us -> 1.3 us
    pallas_call x2 -> x1, Pallas kernels: 78.1 us -> 50.1 us  [body(): pl.pallas_call(fused_kernel, out_shape=jax.ShapeDtypeStruct((8, 256), jnp...]
    reshape x2 -> x0, local copies, waits for them, and re-layouts: 2.61 us -> none  [the longest x1 1.32 us: body(): counts.reshape(8, 1)]
    unnamed x0 -> x1, local copies, waits for them, and re-layouts: none -> 1.3 us
where the time goes in v3:
time: 53.8 us; the launch traced here: 53.6 us
  Pallas kernels  50.1 us (93%)
  other arithmetic  2.14 us (4%)
  local copies, waits for them, and re-layouts  1.3 us (2%)
    pallas_call x1, Pallas kernels, body(): pl.pallas_call(fused_kernel, out_shape=jax.ShapeDtypeStruct((8, 256), jnp...  50.1 us
    convert_element_type x1, other arithmetic, unit_rows(): (values * lax.rsqrt(jnp.sum(values * values, axis=-1, keepdims=True) + EP...  1.36 us
    unnamed x1, local copies, waits for them, and re-layouts  1.3 us

profile of v3, /device:TPU:1, one launch (start us, length us, event | category | flops | bytes accessed | tf_op | source)
XLA Modules:
  0.0 53.6 jit_solution(1157473683650917979)
XLA Ops:
  0.0 0.8 %fusion = f32[8,2]{1,0:T(8,128)S(1)} fusion(bf16[8,2,128]{2,1,0:T(2,128)(2,1)} %param.8), kind=kLoop, calls=%fused_computation.2 | loop fusion | flops 6128 | bytes 4160 | tf_op jit(solution)/shard_map/reduce_sum | solution.py:21
  0.8 1.4 %fusion.1 = bf16[8,2,128]{2,1,0:T(2,128)(2,1)} fusion(bf16[8,2,128]{2,1,0:T(2,128)(2,1)} %param.8, f32[8,2]{1,0:T(8,128)S(1)} %add_rsqrt_fusion), kind=kLoop, calls=%fused_computation.3 | loop fusion | flops 6144 | bytes 8256 | tf_op jit(solution)/shard_map/convert_element_type | solution.py:21
  2.1 50.1 %gather_maxsim.1 = f32[8,256]{1,0:T(8,128)} custom-call(bf16[16,128]{1,0:T(8,128)(2,1)} %bitcast.1, bf16[1920,768]{1,0:T(8,128)(2,1)} %hidden.1, s32[8]{0:T(128)} %counts.1, bf16[768,128]{1,0:T(8,128)(2,1)} %w_proj.1), custom_call_target="tpu_custom_call" | custom-call | tf_op jit(solution)/shard_map/gather_maxsim/pallas_call | solution.py:256
  52.3 1.3 %copy.6 = f32[8,256]{1,0:T(8,128)} copy(f32[8,256]{1,0:T(8,128)} %gather_maxsim.1) | data formatting | bytes 16384
  (1 shorter events, 0.0 us)

commit v4 on v3

--- a/solution.py
+++ b/solution.py
@@ -79,12 +79,13 @@
 
 
 def fused_kernel(
-    own, hidden, counts, w_proj, out,
-    buf, rows_in, vectors, member, totals, even, odd,
+    seeds, hidden, counts, w_proj, out,
+    own, buf, rows_in, vectors, member, totals, even, odd,
     local_sem, hidden_sem, send_z, recv_z, send_h, recv_h, send_c, recv_c,
 ):
     fetch = pltpu.make_async_copy(hidden, rows_in, hidden_sem)
     fetch.start()
+    own[...] = unit_rows(seeds[...].astype(jnp.float32).reshape(16, D))
     me_s = lax.axis_index("shard")
     me_l = lax.axis_index("loop")
     core, y, x_lo = me_s % 2, (me_s // 2) % NY, me_s // (2 * NY)
@@ -216,21 +217,25 @@
     for half in halves:
         first_opposite(half)
     score(-1, 0)
-    for half in halves:
-        second_opposite(half, 0)
-    score(0, 1)
     for half, side in slabs:
         second_arrived(half, side)
+    score(0, 1)
     score(0, -1)
+    score(1, 1)
     for half in halves:
         second_arrived(half, 2)
-    score(2, 0)
+    score(1, -1)
+    for half in halves:
+        second_opposite(half, 0)
+    score(-1, 1)
+    score(-1, -1)
     for half, side in slabs:
         second_opposite(half, side)
-    score(0, 2)
+    for dx, dy in ((2, 0), (0, 2), (2, 1), (2, -1)):
+        score(dx, dy)
     for half in halves:
         second_opposite(half, 2)
-    for dx, dy in ((1, 1), (1, -1), (-1, 1), (-1, -1), (2, 1), (2, -1), (1, 2), (-1, 2), (2, 2)):
+    for dx, dy in ((1, 2), (-1, 2), (2, 2)):
         score(dx, dy)
     drained(None, None, scratch[(len(done) - 1) % 2])
     pairs = (
@@ -250,7 +255,6 @@
 
 
 def body(hidden, segment, counts, w_proj, seeds):
-    block = unit_rows(seeds).reshape(16, D)
     vmem = pl.BlockSpec(memory_space=pltpu.VMEM)
     dma = pltpu.SemaphoreType.DMA
     return pl.pallas_call(
@@ -264,6 +268,7 @@
         ],
         out_specs=vmem,
         scratch_shapes=[
+            pltpu.VMEM((16, D), jnp.bfloat16),
             pltpu.VMEM((SHARDS, LOOPS, 16, D), jnp.bfloat16),
             pltpu.VMEM((ROWS, D_IN), jnp.bfloat16),
             pltpu.VMEM((ROWS, D), jnp.bfloat16),
@@ -284,7 +289,7 @@
             collective_id=0, has_side_effects=True, vmem_limit_bytes=VMEM_LIMIT
         ),
         name="gather_maxsim",
-    )(block, hidden, counts, w_proj)
+    )(seeds, hidden, counts, w_proj)
 
 
 def solution(mesh):

time: 53.8 us -> 51.6 us (0.959)
  other arithmetic: 2.14 us -> 0 us
    convert_element_type x1 -> x0, other arithmetic: 1.36 us -> none  [unit_rows(): (values * lax.rsqrt(jnp.sum(values * values, axis=-1, keepdims=True) + EP...]
    reduce_sum x1 -> x0, other arithmetic: 0.77 us -> none  [unit_rows(): jnp.sum(values * values, axis=-1, keepdims=True) + EPS]
where the time goes in v4:
time: 51.6 us; the launch traced here: 51.4 us
  Pallas kernels  50.1 us (97%)
  local copies, waits for them, and re-layouts  1.3 us (3%)
    pallas_call x1, Pallas kernels, body(): pl.pallas_call(fused_kernel, out_shape=jax.ShapeDtypeStruct((8, 256), jnp...  50.1 us
    unnamed x1, local copies, waits for them, and re-layouts  1.3 us

profile of v4, /device:TPU:1, one launch (start us, length us, event | category | flops | bytes accessed | tf_op | source)
XLA Modules:
  0.0 51.4 jit_solution(16580328944979965403)
XLA Ops:
  0.0 50.1 %gather_maxsim.1 = f32[8,256]{1,0:T(8,128)} custom-call(bf16[8,2,128]{2,1,0:T(2,128)(2,1)} %seeds.1, bf16[1920,768]{1,0:T(8,128)(2,1)} %hidden.1, s32[8]{0:T(128)} %counts.1, bf16[768,128]{1,0:T(8,128)(2,1)} %w_proj.1), custom_call_target="tpu_custom_call" | custom-call | tf_op jit(solution)/shard_map/gather_maxsim/pallas_call | solution.py:260
  50.1 1.3 %copy.6 = f32[8,256]{1,0:T(8,128)} copy(f32[8,256]{1,0:T(8,128)} %gather_maxsim.1) | data formatting | bytes 16384

commit v5 on v4

--- a/solution.py
+++ b/solution.py
@@ -24,7 +24,7 @@
 
 
 COLS = 512
-CHUNKS = [(start, min(256, ROWS - start)) for start in range(0, ROWS, 256)]
+CHUNKS = [(start, min(512, ROWS - start)) for start in range(0, ROWS, 512)]
 
 
 def similarity(vectors, block, start, size):

time: 51.6 us -> 50.2 us (0.973)
  Pallas kernels: 50.1 us -> 48.6 us
    pallas_call x1, Pallas kernels: 50.1 us -> 48.6 us  [body(): pl.pallas_call(fused_kernel, out_shape=jax.ShapeDtypeStruct((8, 256), jnp...]
where the time goes in v5:
time: 50.2 us; the launch traced here: 50 us
  Pallas kernels  48.6 us (97%)
  local copies, waits for them, and re-layouts  1.3 us (3%)
    pallas_call x1, Pallas kernels, body(): pl.pallas_call(fused_kernel, out_shape=jax.ShapeDtypeStruct((8, 256), jnp...  48.6 us
    unnamed x1, local copies, waits for them, and re-layouts  1.3 us

profile of v5, /device:TPU:1, one launch (start us, length us, event | category | flops | bytes accessed | tf_op | source)
XLA Modules:
  0.0 50.0 jit_solution(9800120798235421523)
XLA Ops:
  0.0 48.6 %gather_maxsim.1 = f32[8,256]{1,0:T(8,128)} custom-call(bf16[8,2,128]{2,1,0:T(2,128)(2,1)} %seeds.1, bf16[1920,768]{1,0:T(8,128)(2,1)} %hidden.1, s32[8]{0:T(128)} %counts.1, bf16[768,128]{1,0:T(8,128)(2,1)} %w_proj.1), custom_call_target="tpu_custom_call" | custom-call | tf_op jit(solution)/shard_map/gather_maxsim/pallas_call | solution.py:260
  48.7 1.3 %copy.6 = f32[8,256]{1,0:T(8,128)} copy(f32[8,256]{1,0:T(8,128)} %gather_maxsim.1) | data formatting | bytes 16384
